TPU v7x, 256 devices: a whole 4x4x8 slice. The times are simulated.
256 devices in a mesh: rep: 32 (over z, y), ch: 8 (over x, core).
Axes of the slice: x: 4, y: 4, z: 8, core: 2. Of those that a mesh axis runs over, the one named last changes fastest.
Arguments:
- patches: bfloat16 [32, 768, 4352], P('rep', 'ch'), may hold values from -28 to 28
- cotangents: bfloat16 [32, 768, 2688], P('rep', 'ch'), may hold values from -0.06 to 0.06
- weight: float32 [768, 27, 768], P(('ch', 'rep')), may hold values from -0.0390625 to 0.0390625
- momentum: float32 [768, 27, 768], P(('ch', 'rep')), may hold values from -6 to 6
Outputs:
- new_weight: float32 [768, 27, 768], P(('ch', 'rep'))
- new_momentum: float32 [768, 27, 768], P(('ch', 'rep'))
All inputs are finite; a program needn't handle non-finite values.
Results may differ from a plain program's by a relative error of at most 0.0003.
Values may be sent and summed in bfloat16 or wider, within the bound.
A program may use at most 128 MiB of HBM per device.

v0:
```python
import jax
import jax.numpy as jnp
from jax import lax
from jax.sharding import PartitionSpec as P

KERNEL = 3
DEPTH = 6
HEIGHT = 14
WIDTH = 32


momentum_decay = 0.9
learning_rate = 0.05


def from_partner(value, axis, bit):
    mask = 2**bit
    pairs = [(source, source ^ mask) for source in range(lax.axis_size(axis))]
    return lax.ppermute(value, axis, pairs)


def from_everyone(x, axis):
    copies = jnp.broadcast_to(x, (lax.axis_size(axis), *x.shape))
    return lax.all_to_all(copies, axis, split_axis=0, concat_axis=0, tiled=True)


def taken_together(x, axis):
    return from_everyone(x, axis).sum(axis=0)


def tap_gradient(patch, cotangent):
    volume = patch.reshape(
        patch.shape[1], 1, DEPTH + KERNEL - 1, HEIGHT + KERNEL - 1, WIDTH + KERNEL - 1
    )
    kernel_like = cotangent.reshape(cotangent.shape[1], 1, DEPTH, HEIGHT, WIDTH)
    result = lax.conv_general_dilated(
        volume,
        kernel_like,
        (1, 1, 1),
        "VALID",
        dimension_numbers=("NCDHW", "OIDHW", "CDHWN"),
        preferred_element_type=jnp.float32,
    )
    return result.reshape(result.shape[0], -1, result.shape[-1])


def group_totals(partial_value, pair_bit, levels):
    for upper_bit in range(pair_bit, levels):
        partial_value = partial_value + from_partner(partial_value, "rep", upper_bit)
    return taken_together(partial_value, "ch")


def adasum_halving(blocks, seg_axis):
    replicas = lax.axis_size("rep")
    levels = replicas.bit_length() - 1
    rep_index = lax.axis_index("rep")
    for section_index in range(levels):
        pair_bit = levels - 1 - section_index
        is_upper = rep_index >> pair_bit & 1 == 1
        midpoint = blocks.shape[seg_axis] // 2
        lower_part = lax.slice_in_dim(blocks, 0, midpoint, axis=seg_axis)
        upper_part = lax.slice_in_dim(blocks, midpoint, 2 * midpoint, axis=seg_axis)
        retained = jnp.where(is_upper, upper_part, lower_part)
        outgoing = jnp.where(is_upper, lower_part, upper_part)
        received = from_partner(outgoing, "rep", pair_bit)
        former = jnp.where(is_upper, received, retained)
        latter = jnp.where(is_upper, retained, received)
        partial_value = jnp.stack(
            [jnp.sum(former * latter), jnp.sum(former * former), jnp.sum(latter * latter)]
        )
        totals = group_totals(partial_value, pair_bit, levels)
        blocks = (1.0 - totals[0] / (2.0 * totals[1])) * former + (
            1.0 - totals[0] / (2.0 * totals[2])
        ) * latter
    return blocks


def shards(patches, cotangents, weight, momentum):
    replicas = lax.axis_size("rep")
    tap_count = weight.shape[1]
    gradient = tap_gradient(lax.all_gather(patches, "ch", axis=1, tiled=True), cotangents)
    blocks = gradient.reshape(replicas, -1, tap_count, gradient.shape[2])
    combined = adasum_halving(blocks, 0).reshape(weight.shape)
    new_momentum = momentum_decay * momentum + combined
    new_weight = weight - learning_rate * new_momentum
    return (new_weight, new_momentum)


def solution(mesh):
    in_specs = (
        P("rep", "ch", None),
        P("rep", "ch", None),
        P(("ch", "rep"), None, None),
        P(("ch", "rep"), None, None),
    )
    out_specs = (P(("ch", "rep"), None, None), P(("ch", "rep"), None, None))
    return jax.shard_map(shards, mesh=mesh, in_specs=in_specs, out_specs=out_specs, check_vma=False)
```

profile of v0, /device:TPU:1, one launch (start us, length us, event | category | flops | bytes accessed | tf_op | source)
XLA Modules:
  0.0 763.0 jit_solution(1237505205257916798)
XLA Ops:
  9.3 49.7 %all-gather.2.cloned.1.call-done = bf16[1,768,4352]{2,1,0:T(8,128)(2,1)} async-done(((bf16[1,96,4352]{2,1,0:T(8,128)(2,1)}), bf16[1,768,4352]{2,1,0:T(8,128)(2,1)}) %all-gather.2.cloned.1.call-update) | async-done | bytes 6684688 | tf_op jit(solution)/shard_map/all_gather | solution.py:81
  59.1 9.8 %copy.85 = bf16[1,768,4352]{1,2,0:T(8,128)(2,1)} copy(bf16[1,768,4352]{2,1,0:T(8,128)(2,1)} %all-gather.2.cloned.1.call-done) | data formatting | bytes 13369344 | tf_op jit(solution)/shard_map/all_gather | solution.py:81
  68.8 36.6 %reshape.92 = bf16[768,1,8,16,34]{0,1,4,3,2:T(2,128)(2,1)} reshape(bf16[1,768,4352]{1,2,0:T(8,128)(2,1)} %copy.85) | data formatting | bytes 13369344 | tf_op jit(solution)/shard_map/reshape | solution.py:32
  105.4 107.9 %fusion = f32[96,3,3,3,768]{4,0,3,2,1:T(8,128)S(1)} fusion(bf16[768,1,8,16,34]{0,1,4,3,2:T(2,128)(2,1)} %reshape.92, bf16[96,1,6,14,32]{0,4,3,2,1:T(8,128)(2,1)S(1)} %bitcast.40), kind=kOutput, calls=%fused_computation.16 | convolution fusion | flops 10701766656 | bytes 15163392 | tf_op jit(solution)/shard_map/conv_general_dilated | solution.py:36
  213.3 3.8 slice_select_fusion.1
  217.1 7.2 select_n.115
  224.4 5.2 copy.89
  229.5 5.5 collective-permute-start
  235.0 7.2 select_n.117
  242.2 165.9 %collective-permute-done = f32[16,3,27,768]{3,0,2,1:T(8,128)} collective-permute-done((f32[16,3,27,768]{3,0,2,1:T(8,128)}, f32[16,3,27,768]{3,0,2,1:T(8,128)}, u32[]{:S(2)}, u32[]{:S(2)}) %collective-permute-start) | collective-permute-done | bytes 3981344 | tf_op jit(solution)/shard_map/ppermute | solution.py:19
  408.1 7.6 multiply_reduce_fusion.2
  417.7 5.6 collective-permute-start.1
  426.8 5.2 all-to-all-start
  432.0 4.5 all-to-all-done
  439.8 6.9 multiply_add_fusion
  450.8 88.3 %collective-permute-done.2 = f32[8,3,27,768]{3,0,2,1:T(8,128)S(1)} collective-permute-done((f32[8,3,27,768]{3,0,2,1:T(8,128)}, f32[8,3,27,768]{3,0,2,1:T(8,128)S(1)}, u32[]{:S(2)}, u32[]{:S(2)}) %collective-permute-start.2) | collective-permute-done | bytes 1990688 | tf_op jit(solution)/shard_map/ppermute | solution.py:19
  539.1 6.4 multiply_reduce_fusion.5
  552.9 4.6 collective-permute-start.4
  561.9 6.2 all-to-all-start.1
  568.1 4.5 all-to-all-done.1
  580.9 23.2 %collective-permute-done.5 = f32[4,3,27,768]{3,0,2,1:T(4,128)} collective-permute-done((f32[4,3,27,768]{3,0,2,1:T(4,128)}, f32[4,3,27,768]{3,0,2,1:T(4,128)}, u32[]{:S(2)}, u32[]{:S(2)}) %collective-permute-start.5) | collective-permute-done | bytes 995360 | tf_op jit(solution)/shard_map/ppermute | solution.py:19
  604.1 4.4 multiply_reduce_fusion.8
  620.5 4.6 collective-permute-start.8
  627.5 8.2 %all-to-all-start.2 = ((f32[8,1,3]{2,1,0:T(1,128)}), f32[8,1,3]{2,1,0:T(1,128)S(1)}, u32[]{:S(2)}, u32[]{:S(2)}) async-start(f32[8,1,3]{2,1,0:T(1,128)} %broadcast_in_dim.17), calls=%async_computation.2 | async-start | bytes 8192 | tf_op jit(solution)/shard_map/all_to_all | solution.py:24
  635.7 4.5 all-to-all-done.2
  648.8 11.0 %collective-permute-done.9 = f32[2,3,27,768]{3,0,2,1:T(2,128)S(1)} collective-permute-done((f32[2,3,27,768]{3,0,2,1:T(2,128)S(1)}, f32[2,3,27,768]{3,0,2,1:T(2,128)S(1)}, u32[]{:S(2)}, u32[]{:S(2)}) %collective-permute-start.9) | collective-permute-done | bytes 497696 | tf_op jit(solution)/shard_map/ppermute | solution.py:19
  677.2 4.6 collective-permute-start.13
  684.1 9.4 %all-to-all-start.3 = ((f32[8,1,3]{2,1,0:T(1,128)}), f32[8,1,3]{2,1,0:T(1,128)S(1)}, u32[]{:S(2)}, u32[]{:S(2)}) async-start(f32[8,1,3]{2,1,0:T(1,128)} %broadcast_in_dim.18), calls=%async_computation.3 | async-start | bytes 8192 | tf_op jit(solution)/shard_map/all_to_all | solution.py:24
  693.4 4.5 all-to-all-done.3
  702.9 7.5 collective-permute-done.14
  729.9 4.6 collective-permute-start.19
  736.3 14.2 %all_to_all.30 = f32[8,1,3]{2,1,0:T(1,128)S(1)} all-to-all(f32[8,1,3]{2,1,0:T(1,128)S(1)} %broadcast_in_dim.19), channel_id=1, replica_groups=mesh['rep'=32,'ch'=8] {'ch'}, dimensions={0} | all-to-all | bytes 192 | tf_op jit(solution)/shard_map/all_to_all | solution.py:24
  (88 shorter events, 96.1 us)
Async XLA Ops:
  7.2 51.9 %all-gather.2.cloned.1.call-start = ((), (), s32[]{:S(2)}) async-start(), calls=%async_computation.5 | async-start | bytes 7520256 | tf_op jit(solution)/shard_map/all_gather | solution.py:81
  229.5 178.6 %collective-permute-start = (f32[16,3,27,768]{3,0,2,1:T(8,128)}, f32[16,3,27,768]{3,0,2,1:T(8,128)}, u32[]{:S(2)}, u32[]{:S(2)}) collective-permute-start(f32[16,3,27,768]{3,0,2,1:T(8,128)} %copy.89), channel_id=1, source_target_pairs={{0,128},{8,136},{16,144},{24,152},{32,160},{40,168},{48,176},{56,1... | collective-permute-start | bytes 11943944 | tf_op jit(solution)/shard_map/ppermute | solution.py:19
  417.7 6.6 collective-permute-start.1
  426.8 9.8 %all-to-all-start = ((f32[8,1,3]{2,1,0:T(1,128)}), f32[8,1,3]{2,1,0:T(1,128)S(1)}, u32[]{:S(2)}, u32[]{:S(2)}) async-start(f32[8,1,3]{2,1,0:T(1,128)} %broadcast_in_dim.15), calls=%async_computation | async-start | bytes 8192 | tf_op jit(solution)/shard_map/all_to_all | solution.py:24
  446.8 2.3 copy-start
  450.8 88.3 %collective-permute-start.2 = (f32[8,3,27,768]{3,0,2,1:T(8,128)}, f32[8,3,27,768]{3,0,2,1:T(8,128)S(1)}, u32[]{:S(2)}, u32[]{:S(2)}) collective-permute-start(f32[8,3,27,768]{3,0,2,1:T(8,128)} %copy.93), channel_id=1, source_target_pairs={{0,64},{8,72},{16,80},{24,88},{32,96},{40,104},{48,112},{56,120},{... | collective-permute-start | bytes 5971976 | tf_op jit(solution)/shard_map/ppermute | solution.py:19
  547.5 3.3 collective-permute-start.3
  552.9 6.4 collective-permute-start.4
  561.9 10.7 %all-to-all-start.1 = ((f32[8,1,3]{2,1,0:T(1,128)}), f32[8,1,3]{2,1,0:T(1,128)S(1)}, u32[]{:S(2)}, u32[]{:S(2)}) async-start(f32[8,1,3]{2,1,0:T(1,128)} %broadcast_in_dim.16), calls=%async_computation.1 | async-start | bytes 8192 | tf_op jit(solution)/shard_map/all_to_all | solution.py:24
  580.9 23.2 %collective-permute-start.5 = (f32[4,3,27,768]{3,0,2,1:T(4,128)}, f32[4,3,27,768]{3,0,2,1:T(4,128)}, u32[]{:S(2)}, u32[]{:S(2)}) collective-permute-start(f32[4,3,27,768]{3,0,2,1:T(4,128)} %copy.97), channel_id=1, source_target_pairs={{0,32},{8,40},{16,48},{24,56},{32,0},{40,8},{48,16},{56,24},{64,96... | collective-permute-start | bytes 2985992 | tf_op jit(solution)/shard_map/ppermute | solution.py:19
  610.6 2.4 collective-permute-start.6
  615.1 3.3 collective-permute-start.7
  620.5 6.4 collective-permute-start.8
  627.5 12.8 %all-to-all-start.2 = ((f32[8,1,3]{2,1,0:T(1,128)}), f32[8,1,3]{2,1,0:T(1,128)S(1)}, u32[]{:S(2)}, u32[]{:S(2)}) async-start(f32[8,1,3]{2,1,0:T(1,128)} %broadcast_in_dim.17), calls=%async_computation.2 | async-start | bytes 8192 | tf_op jit(solution)/shard_map/all_to_all | solution.py:24
  645.9 13.8 %collective-permute-start.9 = (f32[2,3,27,768]{3,0,2,1:T(2,128)S(1)}, f32[2,3,27,768]{3,0,2,1:T(2,128)S(1)}, u32[]{:S(2)}, u32[]{:S(2)}) collective-permute-start(f32[2,3,27,768]{3,0,2,1:T(2,128)S(1)} %copy.101), channel_id=1, source_target_pairs={{0,16},{8,24},{16,0},{24,8},{32,48},{40,56},{48,32},{56,40},{64,80... | collective-permute-start | bytes 1493000 | tf_op jit(solution)/shard_map/ppermute | solution.py:19
  661.2 92.7 %copy-start.1 = (f32[3,27,768]{2,1,0:T(8,128)S(1)}, f32[3,27,768]{2,1,0:T(8,128)}, u32[]{:S(2)}) copy-start(f32[3,27,768]{2,1,0:T(8,128)} %param.6) | copy-start | bytes 746500
  661.2 92.7 %copy-start.2 = (f32[3,27,768]{2,1,0:T(8,128)S(1)}, f32[3,27,768]{2,1,0:T(8,128)}, u32[]{:S(2)}) copy-start(f32[3,27,768]{2,1,0:T(8,128)} %param.7) | copy-start | bytes 746500
  663.3 4.0 collective-permute-start.10
  669.3 2.4 collective-permute-start.11
  673.8 3.3 collective-permute-start.12
  677.2 6.3 collective-permute-start.13
  684.1 13.9 %all-to-all-start.3 = ((f32[8,1,3]{2,1,0:T(1,128)}), f32[8,1,3]{2,1,0:T(1,128)S(1)}, u32[]{:S(2)}, u32[]{:S(2)}) async-start(f32[8,1,3]{2,1,0:T(1,128)} %broadcast_in_dim.18), calls=%async_computation.3 | async-start | bytes 8192 | tf_op jit(solution)/shard_map/all_to_all | solution.py:24
  701.6 8.7 %collective-permute-start.14 = (f32[1,3,27,768]{3,1,0,2:T(4,128)S(1)}, f32[1,3,27,768]{3,1,0,2:T(4,128)S(1)}, u32[]{:S(2)}, u32[]{:S(2)}) collective-permute-start(f32[1,3,27,768]{3,1,0,2:T(4,128)S(1)} %slice_select_fusion.9), channel_id=1, source_target_pairs={{0,8},{8,0},{16,24},{24,16},{32,40},{40,32},{48,56},{56,48},{64,72... | collective-permute-start | bytes 746504 | tf_op jit(solution)/shard_map/ppermute | solution.py:19
  713.4 2.4 collective-permute-start.15
  717.9 4.2 collective-permute-start.16
  724.2 2.4 collective-permute-start.17
  726.6 3.3 collective-permute-start.18
  729.9 6.3 collective-permute-start.19
Sparse Core Ops, SparseCore 0:
  9.8 49.2 all-gather.1
where the time goes:
time: 778 us; the launch traced here: 763 us
  waiting for transfers between devices  396 us (51%)
  matrix products  108 us (14%)
  local copies, waits for them, and re-layouts  79 us (10%)
  starting transfers between devices  70 us (9%)
  other arithmetic  68.1 us (9%)
  between operations  27.5 us (4%)
  blocking collectives  14.2 us (2%)
    ppermute x20, waiting for transfers between devices, from_partner(): return lax.ppermute(value, axis, pairs)  328 us
    conv_general_dilated x1, matrix products, tap_gradient(): lax.conv_general_dilated(volume, kernel_like, (1, 1, 1), 'VALID', dimensi...  108 us
    all_gather x1, waiting for transfers between devices, shards(): lax.all_gather(patches, 'ch', axis=1, tiled=True)  49.7 us
    ppermute x20, starting transfers between devices, from_partner(): return lax.ppermute(value, axis, pairs)  40.9 us
    reshape x1, local copies, waits for them, and re-layouts, tap_gradient(): patch.reshape(patch.shape[1], 1, DEPTH + KERNEL - 1, HEIGHT + KERNEL - 1,...  36.6 us
    all_to_all x4, starting transfers between devices, from_everyone(): return lax.all_to_all(copies, axis, split_axis=0, concat_axis=0, tiled=True)  29 us
    reduce_sum x5, other arithmetic, adasum_halving(): jnp.sum(former * latter)  20.9 us
    add x15, other arithmetic, group_totals(): partial_value + from_partner(partial_value, 'rep', upper_bit)  18.4 us
  transfers between devices with their start and end apart: 25, of which 25 were waited for; matrix products, arithmetic and copies ran while one was open for 1% of the time, Pallas kernels for 0%

commit v1 on v0

v1 whole, which is shorter than its diff:
```python
import jax
import jax.numpy as jnp
from jax import lax
from jax.experimental import pallas as pl
from jax.experimental.pallas import tpu as pltpu
from jax.sharding import PartitionSpec as P

KERNEL = 3
DEPTH = 6
HEIGHT = 14
WIDTH = 32
ROW = WIDTH + KERNEL - 1
PLANE = (HEIGHT + KERNEL - 1) * ROW
CELLS = (DEPTH + KERNEL - 1) * PLANE
VOX = DEPTH * HEIGHT * WIDTH

Z = 8
Y = 4
Z_GROUPS = [[4 * z + y for z in range(Z)] for y in range(Y)]
Y_GROUPS = [[4 * z + y for y in range(Y)] for z in range(Z)]

momentum_decay = 0.9
learning_rate = 0.05


def grads_kernel(d_ref, p_ref, g_ref, k_ref, s_ref, ps_ref):
    r = pl.program_id(0)

    @pl.when(r == 0)
    def _():
        s_ref[...] = jnp.zeros_like(s_ref)

    for i in range(DEPTH):
        for j in range(HEIGHT):
            src = d_ref[0, :, pl.ds((i * HEIGHT + j) * WIDTH, WIDTH)]
            for a in range(KERNEL):
                s_ref[a * 96 : (a + 1) * 96, pl.ds((a + i) * PLANE + j * ROW, WIDTH)] = src
    for b in range(KERNEL):
        for e in range(KERNEL):
            s = ROW * b + e
            row = (b * KERNEL + e) * 96
            if s == 0:
                ps_ref[row : row + 96, :] = p_ref[0]
            else:
                ps_ref[row : row + 96, : CELLS - s] = p_ref[0, :, s:]
                ps_ref[row : row + 96, CELLS - s :] = jnp.zeros((96, s), jnp.bfloat16)
    g_ref[r] = lax.dot_general(
        s_ref[...], ps_ref[...], (((1,), (1,)), ((), ())), preferred_element_type=jnp.float32
    )
    for q in range(Z):

        @pl.when(q <= r)
        def _():
            k_ref[r, q] = jnp.sum(g_ref[r] * g_ref[q])

        @pl.when(q > r)
        def _():
            k_ref[r, q] = 0.0


def grads(d, p):
    return pl.pallas_call(
        grads_kernel,
        grid=(Z,),
        in_specs=[
            pl.BlockSpec((1, 96, VOX), lambda r: (r, 0, 0)),
            pl.BlockSpec((1, 96, CELLS), lambda r: (r, 0, 0)),
        ],
        out_specs=[
            pl.BlockSpec((Z, 288, 864), lambda r: (0, 0, 0), pipeline_mode=pl.Buffered(1)),
            pl.BlockSpec(memory_space=pltpu.SMEM),
        ],
        out_shape=[
            jax.ShapeDtypeStruct((Z, 288, 864), jnp.float32),
            jax.ShapeDtypeStruct((Z, Z), jnp.float32),
        ],
        scratch_shapes=[
            pltpu.VMEM((288, CELLS), jnp.bfloat16),
            pltpu.VMEM((864, CELLS), jnp.bfloat16),
        ],
        compiler_params=pltpu.CompilerParams(vmem_limit_bytes=56 * 2**20),
    )(d, p)


def tree_weights(gram):
    n = gram.shape[0]
    coef = jnp.eye(n, dtype=jnp.float32)
    while n > 1:
        n //= 2
        lo, hi = coef[:n], coef[n:]
        gram_hi = jnp.sum(hi[:, :, None] * gram[None], axis=1)
        gram_lo = jnp.sum(lo[:, :, None] * gram[None], axis=1)
        inner = jnp.sum(lo * gram_hi, axis=1)
        lo_sq = jnp.sum(lo * gram_lo, axis=1)
        hi_sq = jnp.sum(hi * gram_hi, axis=1)
        coef = (1.0 - inner / (2.0 * lo_sq))[:, None] * lo + (1.0 - inner / (2.0 * hi_sq))[:, None] * hi
    return coef[0]


def shards(patches, cotangents, weight, momentum):
    d = cotangents[0].reshape(Z, Y, 3, VOX).transpose(1, 0, 2, 3).reshape(96, VOX)
    d = lax.all_gather(d, "rep", axis_index_groups=Z_GROUPS)
    p = patches[0].reshape(Z, 12, CELLS)
    p = lax.all_to_all(p, "rep", 0, 0, axis_index_groups=Z_GROUPS, tiled=True)
    p = lax.all_gather(p, "ch", axis=1, tiled=True)
    g, gram = grads(d, p)
    gram = lax.psum(lax.psum(gram, "ch"), "rep", axis_index_groups=Z_GROUPS)
    gram = gram + jnp.tril(gram, -1).T
    w = tree_weights(gram)
    v = jnp.sum(w[:, None, None] * g, axis=0)
    v = v.reshape(KERNEL, Y, 24, 864)
    v = lax.all_to_all(v, "rep", 1, 0, axis_index_groups=Y_GROUPS)
    gram = jnp.stack([jnp.stack([jnp.sum(v[i] * v[j]) for j in range(Y)]) for i in range(Y)])
    gram = lax.psum(gram, ("rep", "ch"))
    w = tree_weights(gram)
    v = jnp.sum(w[:, None, None, None] * v, axis=0)
    v = v.reshape(KERNEL, Z, 3, 864)
    v = lax.all_to_all(v, "rep", 1, 0, axis_index_groups=Z_GROUPS)
    v = v.reshape(Z, KERNEL, 3, 9, 8, 12).transpose(2, 1, 3, 4, 0, 5).reshape(weight.shape)
    new_momentum = momentum_decay * momentum + v
    new_weight = weight - learning_rate * new_momentum
    return (new_weight, new_momentum)


def solution(mesh):
    in_specs = (
        P("rep", "ch", None),
        P("rep", "ch", None),
        P(("ch", "rep"), None, None),
        P(("ch", "rep"), None, None),
    )
    out_specs = (P(("ch", "rep"), None, None), P(("ch", "rep"), None, None))
    return jax.shard_map(shards, mesh=mesh, in_specs=in_specs, out_specs=out_specs, check_vma=False)
```

time: 778 us -> 386 us (0.50); the launches traced: 763 us -> 385 us
  waiting for transfers between devices: 396 us -> 100 us
  blocking collectives: 14.2 us -> 157 us
  matrix products: 108 us -> 0 us
  Pallas kernels: 0 us -> 66.8 us
  starting transfers between devices: 70 us -> 4.08 us
  local copies, waits for them, and re-layouts: 79 us -> 19.7 us
  other arithmetic: 68.1 us -> 17.5 us
  between operations: 27.5 us -> 19.4 us
    ppermute x20 -> x0, waiting for transfers between devices: 328 us -> none  [from_partner(): return lax.ppermute(value, axis, pairs)]
    conv_general_dilated x1 -> x0, matrix products: 108 us -> none  [tap_gradient(): lax.conv_general_dilated(volume, kernel_like, (1, 1, 1), 'VALID', dimensi...]
    psum x0 -> x3, blocking collectives: none -> 103 us  [the longest x1 79 us: shards(): gram = lax.psum(gram, ('rep', 'ch'))]
    pallas_call x0 -> x1, Pallas kernels: none -> 66.8 us  [grads(): pl.pallas_call(grads_kernel, grid=(Z,), in_specs=[pl.BlockSpec((1, 96, VO...]
    ppermute x20 -> x0, starting transfers between devices: 40.9 us -> none  [from_partner(): return lax.ppermute(value, axis, pairs)]
    all_gather x1 -> x2, waiting for transfers between devices: 49.7 us -> 90.4 us  [the longest x1 48.6 us: shards(): d = lax.all_gather(d, 'rep', axis_index_groups=Z_GROUPS)]
    all_to_all x1 -> x2, blocking collectives: 14.2 us -> 53.6 us  [the longest x1 37.6 us: shards(): p = lax.all_to_all(p, 'rep', 0, 0, axis_index_groups=Z_GROUPS, tiled=True)]
    reshape x1, local copies, waits for them, and re-layouts: 36.6 us -> 4.03 us  [shards(): v.reshape(Z, KERNEL, 3, 9, 8, 12).transpose(2, 1, 3, 4, 0, 5)]
  transfers between devices with their start and end apart: 25 -> 3, of which waited for: 25 -> 3; matrix products, arithmetic and copies ran while one was open for 1% -> 2% of each run, Pallas kernels for 0% -> 0%
where the time goes in v1:
time: 386 us; the launch traced here: 385 us
  blocking collectives  157 us (41%)
  waiting for transfers between devices  100 us (26%)
  Pallas kernels  66.8 us (17%)
  local copies, waits for them, and re-layouts  19.7 us (5%)
  between operations  19.4 us (5%)
  other arithmetic  17.5 us (5%)
  starting transfers between devices  4.08 us (1%)
    psum x1, blocking collectives, shards(): gram = lax.psum(gram, ('rep', 'ch'))  79 us
    pallas_call x1, Pallas kernels, grads(): pl.pallas_call(grads_kernel, grid=(Z,), in_specs=[pl.BlockSpec((1, 96, VO...  66.8 us
    all_gather x1, waiting for transfers between devices, shards(): d = lax.all_gather(d, 'rep', axis_index_groups=Z_GROUPS)  48.6 us
    all_gather x1, waiting for transfers between devices, shards(): p = lax.all_gather(p, 'ch', axis=1, tiled=True)  41.7 us
    all_to_all x1, blocking collectives, shards(): p = lax.all_to_all(p, 'rep', 0, 0, axis_index_groups=Z_GROUPS, tiled=True)  37.6 us
    psum x2, blocking collectives, shards(): gram = lax.psum(lax.psum(gram, 'ch'), 'rep', axis_index_groups=Z_GROUPS)  24.5 us
    all_to_all x1, blocking collectives, shards(): v = lax.all_to_all(v, 'rep', 1, 0, axis_index_groups=Z_GROUPS)  16 us
    all_to_all x1, waiting for transfers between devices, shards(): v = lax.all_to_all(v, 'rep', 1, 0, axis_index_groups=Y_GROUPS)  9.65 us
  transfers between devices with their start and end apart: 3, of which 3 were waited for; matrix products, arithmetic and copies ran while one was open for 2% of the time, Pallas kernels for 0%

profile of v1, /device:TPU:1, one launch (start us, length us, event | category | flops | bytes accessed | tf_op | source)
XLA Modules:
  0.0 384.6 jit_solution(10083630089295017152)
XLA Ops:
  7.2 1.4 reshape_squeeze.10
  8.6 37.6 %all_to_all.35 = bf16[8,12,4352]{2,1,0:T(8,128)(2,1)S(1)} all-to-all(bf16[8,12,4352]{2,1,0:T(8,128)(2,1)S(1)} %reshape_squeeze.10), channel_id=1, replica_groups={{0,32,64,96,128,160,192,224},{8,40,72,104,136,168,200,232},{16,48,80,11..., dimensions={0} | all-to-all | bytes 1671168 | tf_op jit(solution)/shard_map/all_to_all | solution.py:104
  46.2 1.2 copy.31
  47.4 0.2 reshape_squeeze.9
  47.7 0.2 copy.30
  47.9 1.2 all_gather_reshape.3
  49.2 41.7 %all-gather.5.cloned.1.call-done = bf16[8,96,4352]{2,0,1:T(8,128)(2,1)} async-done(((bf16[8,12,4352]{2,0,1:T(8,128)(2,1)}), bf16[8,96,4352]{2,0,1:T(8,128)(2,1)}) %all-gather.5.cloned.1.call-update) | async-done | bytes 6684688 | tf_op jit(solution)/shard_map/all_gather | solution.py:105
  90.9 6.9 %copy.32.p_ref = bf16[8,96,4352]{2,1,0:T(8,128)(2,1)} copy(bf16[8,96,4352]{2,0,1:T(8,128)(2,1)} %all-gather.5.cloned.1.call-done) | data formatting | bytes 13369344 | tf_op jit(solution)/shard_map/all_gather | solution.py:105
  97.8 48.6 %all-gather.3.cloned.1.call-done.d_ref = bf16[8,96,2688]{2,1,0:T(8,128)(2,1)} async-done(((bf16[1,96,2688]{2,1,0:T(8,128)(2,1)}), bf16[8,96,2688]{2,1,0:T(8,128)(2,1)}) %all-gather.3.cloned.1.call-update) | async-done | bytes 4128784 | tf_op jit(solution)/shard_map/all_gather | solution.py:102
  146.4 66.8 %shard_map.59 = (f32[8,288,864]{2,1,0:T(8,128)}, f32[8,8]{1,0:T(8,128)}) custom-call(bf16[8,96,2688]{2,1,0:T(8,128)(2,1)} %all-gather.3.cloned.1.call-done.d_ref, bf16[8,96,4352]{2,1,0:T(8,128)(2,1)} %copy.32.p_ref), custom_call_target="tpu_custom_call" | custom-call | tf_op jit(solution)/shard_map/pallas_call | solution.py:62
  213.2 12.8 %psum.21 = f32[8,8]{1,0:T(8,128)S(1)} all-reduce(f32[8,8]{1,0:T(8,128)} %get-tuple-element.4), channel_id=1, replica_groups=mesh['rep'=32,'ch'=8] {'ch'}, use_global_device_ids=true, to_apply=%region_0.0 | all-reduce | flops 64 | bytes 512 | tf_op jit(solution)/shard_map/psum | solution.py:107
  226.0 11.8 %psum.22 = f32[8,8]{1,0:T(8,128)S(1)} all-reduce(f32[8,8]{1,0:T(8,128)S(1)} %psum.21), channel_id=1, replica_groups={{0,32,64,96,128,160,192,224},{8,40,72,104,136,168,200,232},{16,48,80,11..., use_global_device_ids=true, to_apply=%region_1.0 | all-reduce | flops 64 | bytes 512 | tf_op jit(solution)/shard_map/psum | solution.py:107
  237.9 0.2 multiply_reduce_fusion.21
  238.3 0.2 multiply_reduce_fusion.27
  238.6 0.6 fusion.8
  241.8 4.1 %multiply_reduce_fusion = f32[288,864]{1,0:T(8,128)S(1)} fusion(f32[8,288,864]{2,1,0:T(8,128)} %get-tuple-element.5, f32[8]{0:T(128)S(1)} %add_bitcast_fusion.1), kind=kLoop, calls=%fused_computation | loop fusion | flops 3732480 | bytes 8957984 | tf_op jit(solution)/shard_map/reduce_sum | solution.py:110
  245.9 1.1 copy.34
  247.0 4.0 %all-to-all-start.1 = ((f32[1,3,4,24,864]{4,3,1,0,2:T(8,128)}), f32[1,3,4,24,864]{4,3,1,0,2:T(8,128)S(1)}, u32[]{:S(2)}, u32[]{:S(2)}) async-start(f32[1,3,4,24,864]{4,3,1,0,2:T(8,128)} %copy.34), calls=%async_computation.1 | async-start | bytes 2064384 | tf_op jit(solution)/shard_map/all_to_all | solution.py:112
  251.0 9.7 %all-to-all-done.1 = f32[1,3,4,24,864]{4,3,1,0,2:T(8,128)S(1)} async-done(((f32[1,3,4,24,864]{4,3,1,0,2:T(8,128)}), f32[1,3,4,24,864]{4,3,1,0,2:T(8,128)S(1)}, u32[]{:S(2)}, u32[]{:S(2)}) %all-to-all-start.1) | async-done | bytes 995360 | tf_op jit(solution)/shard_map/all_to_all | solution.py:112
  260.6 0.9 multiply_reduce_fusion.10
  261.5 4.6 %maximum_bitcast_fusion = (f32[1,4]{1,0:T(1,128)S(1)}, f32[1,4]{1,0:T(1,128)S(1)}) fusion(f32[1]{0:T(128)} %bitcast.14, f32[1]{0:T(128)} %bitcast.13, f32[1]{0:T(128)} %bitcast.12, f32[1]{0:T(128)} %bitcast.10, f32[1]{0:T(128)} %bitcast.18, f32[1]{0:T(128)} %bitcast.17, f32[1]{0:T(128)} %bitcast.16), kind=kLoop, calls=%fused_computation.45 | loop fusion | flops 24 | bytes 60 | tf_op jit(solution)/shard_map/stack | solution.py:113
  266.1 4.4 %maximum_bitcast_fusion.2 = (f32[1,4]{1,0:T(1,128)S(1)}, f32[1,4]{1,0:T(1,128)S(1)}) fusion(f32[1]{0:T(128)} %bitcast.21, f32[1]{0:T(128)} %bitcast.20, f32[1]{0:T(128)} %bitcast.17, f32[1]{0:T(128)} %bitcast.13, f32[1]{0:T(128)} %bitcast.23, f32[1]{0:T(128)} %bitcast.18, f32[1]{0:T(128)} %bitcast.14), kind=kLoop, calls=%fused_computation.47 | loop fusion | flops 24 | bytes 60 | tf_op jit(solution)/shard_map/stack | solution.py:113
  270.5 79.0 %psum.23 = f32[4,4]{1,0:T(4,128)S(1)} all-reduce(f32[4,4]{1,0:T(4,128)S(1)} %pad_maximum_fusion), channel_id=1, replica_groups=mesh['rep'=32,'ch'=8] {'rep','ch'}, use_global_device_ids=true, to_apply=%region_28.29 | all-reduce | flops 16 | bytes 128 | tf_op jit(solution)/shard_map/psum | solution.py:114
  349.5 0.2 multiply_reduce_fusion.24
  349.9 0.7 fusion.5
  353.2 0.1 fusion
  353.5 0.3 copy.35
  353.8 16.0 %all_to_all.36 = f32[1,3,8,3,864]{4,0,3,1,2:T(1,128)S(1)} all-to-all(f32[1,3,8,3,864]{4,0,3,1,2:T(1,128)S(1)} %copy.35), channel_id=1, replica_groups={{0,32,64,96,128,160,192,224},{8,40,72,104,136,168,200,232},{16,48,80,11..., dimensions={2} | all-to-all | bytes 497664 | tf_op jit(solution)/shard_map/all_to_all | solution.py:118
  369.8 0.8 reshape_squeeze.11
  370.7 2.1 copy.37
  372.8 4.0 %reshape.141 = f32[3,27,768]{2,1,0:T(8,128)S(1)} reshape(f32[3,3,9,8,8,12]{5,4,3,2,1,0:T(8,128)} %copy.37) | data formatting | bytes 497664 | tf_op jit(solution)/shard_map/reshape | solution.py:119
  376.8 0.9 multiply_subtract_fusion
  (36 shorter events, 1.1 us)
Async XLA Ops:
  7.2 40.3 %copy-start = (bf16[1,96,2688]{2,1,0:T(8,128)(2,1)S(1)}, bf16[1,96,2688]{2,1,0:T(8,128)(2,1)}, u32[]{:S(2)}) copy-start(bf16[1,96,2688]{2,1,0:T(8,128)(2,1)} %param.5) | copy-start | bytes 1548292
  7.2 83.8 %all-gather.5.cloned.1.call-start = ((), (), s32[]{:S(2)}) async-start(), calls=%async_computation.4 | async-start | bytes 7520256 | tf_op jit(solution)/shard_map/all_gather | solution.py:105
  47.4 99.1 %all-gather.3.cloned.1.call-start = ((), (), s32[]{:S(2)}) async-start(), calls=%async_computation.3 | async-start | bytes 4644864 | tf_op jit(solution)/shard_map/all_gather | solution.py:102
  247.0 13.7 %all-to-all-start.1 = ((f32[1,3,4,24,864]{4,3,1,0,2:T(8,128)}), f32[1,3,4,24,864]{4,3,1,0,2:T(8,128)S(1)}, u32[]{:S(2)}, u32[]{:S(2)}) async-start(f32[1,3,4,24,864]{4,3,1,0,2:T(8,128)} %copy.34), calls=%async_computation.1 | async-start | bytes 2064384 | tf_op jit(solution)/shard_map/all_to_all | solution.py:112
  353.4 23.5 %copy-start.1 = (f32[3,27,768]{2,1,0:T(8,128)S(1)}, f32[3,27,768]{2,1,0:T(8,128)}, u32[]{:S(2)}) copy-start(f32[3,27,768]{2,1,0:T(8,128)} %param.6) | copy-start | bytes 746500
  353.4 23.4 %copy-start.2 = (f32[3,27,768]{2,1,0:T(8,128)S(1)}, f32[3,27,768]{2,1,0:T(8,128)}, u32[]{:S(2)}) copy-start(f32[3,27,768]{2,1,0:T(8,128)} %param.7) | copy-start | bytes 746500
Sparse Core Ops, SparseCore 0:
  47.5 43.3 all-gather.4
  92.7 53.6 all-gather.2
